TPU v7x, 32 devices: a whole 2x2x4 slice. The times are simulated.
32 devices in a mesh: img: 16 (over z, x, core), fou: 2 (over y).
Axes of the slice: x: 2, y: 2, z: 4, core: 2. Of those that a mesh axis runs over, the one named last changes fastest.
Arguments:
- sky_estimate: float32 [4, 2048, 2048], P(None, 'img', 'fou'), may hold values from 0 to 2
- dual_coeffs: bfloat16 [4, 9, 2048, 2048], P(None, None, 'img', 'fou'), may hold values from -2 to 2
- dirty_image: float32 [4, 2048, 2048], P(None, 'img', 'fou'), may hold values from -4 to 4
- filters: float32 [8, 17], replicated, may hold values from -1.5 to 1.5
- thresholds: float32 [9], replicated, may hold values from 0.2 to 1.2
- facet_rows: int32 [16], P('img'), may hold values from 32 to 128, as said below
- tile_slots: int32 [4, 32, 6], P(None, 'img'), may hold values from 0 to 31, as said below
- tile_count: int32 [4, 32], P(None, 'img'), may hold values from 1 to 6, as said below
- gram_tiles: bfloat16 [4, 32, 6, 64, 64], P(None, 'img'), may hold values from -4 to 4
Outputs:
- image_next: float32 [4, 2048, 2048], P(None, 'img', 'fou')
- dual_next: bfloat16 [4, 9, 2048, 2048], P(None, None, 'img', 'fou')
Inputs may be any that keep to these rules, and one draw needn't show every extreme that they name: `facet_rows`: facet f covers image rows f * 128 to (f + 1) * 128 - 1; some facet is full. `tile_slots`: the 6 entries of one channel and v-tile are distinct. `tile_count`: slots at or beyond the count hold no tile; in each channel some v-tile uses all 6 slots.
All inputs are finite; a program needn't handle non-finite values.
Results may differ from a plain program's by a relative error of at most 0.005.
Values may be sent and summed in bfloat16 or wider, within the bound.
A program may use at most 192 MiB of HBM per device.

v0:
```python
import math

import jax
import jax.numpy as jnp
from jax import lax
from jax.sharding import PartitionSpec as P

PIXELS = 2048
RADIUS = 8
BLOCK = 64
SLOTS = 6
FACTOR = 16
BLOCKS = 32


STEP_PRIMAL = 0.5
STEP_DUAL = 0.5
PRECISE = lax.Precision.HIGHEST


def for_sending(shard):
    return jax.tree.map(lambda a: a.astype(jnp.bfloat16) if a.dtype == jnp.float32 else a, shard)


def padded_2(cells, sides, width):
    for axis, dim in sides:
        count = lax.axis_size(axis)
        ends = count - 1
        head = lax.slice_in_dim(cells, 0, width, axis=dim)
        tail = lax.slice_in_dim(cells, cells.shape[dim] - width, cells.shape[dim], axis=dim)
        cells = jnp.concatenate(
            [
                lax.ppermute(tail, axis, [(i, (i + 1) % count) for i in range(ends)]),
                cells,
                lax.ppermute(head, axis, [((i + 1) % count, i) for i in range(ends)]),
            ],
            axis=dim,
        )
    return cells


def spin_tables(length, direction):
    counter = jnp.arange(length, dtype=jnp.int32)
    angles = (counter[:, None] * counter[None, :] % length).astype(jnp.float32) * (
        2.0 * math.pi / length
    )
    return (jnp.cos(angles), direction * jnp.sin(angles))


def transform_final_axis(part_re, part_im, direction):
    line_len = part_re.shape[-1]
    inner_len = line_len // FACTOR
    leading = part_re.shape[:-1]
    cos_outer, sin_outer = spin_tables(FACTOR, direction)
    cos_inner, sin_inner = spin_tables(inner_len, direction)
    outer_index = jnp.arange(FACTOR, dtype=jnp.int32)[:, None]
    inner_index = jnp.arange(inner_len, dtype=jnp.int32)[None, :]
    twiddle = (outer_index * inner_index % line_len).astype(jnp.float32) * (
        2.0 * math.pi / line_len
    )
    twiddle_cos = jnp.cos(twiddle)
    rotation_sine = direction * jnp.sin(twiddle)
    shaped_re = part_re.reshape(leading + (FACTOR, inner_len))
    first_re = jnp.einsum("pa,...ab->...pb", cos_outer, shaped_re, precision=PRECISE)
    first_im = jnp.einsum("pa,...ab->...pb", sin_outer, shaped_re, precision=PRECISE)
    if part_im is not None:
        shaped_im = part_im.reshape(leading + (FACTOR, inner_len))
        first_re = first_re - jnp.einsum("pa,...ab->...pb", sin_outer, shaped_im, precision=PRECISE)
        first_im = first_im + jnp.einsum("pa,...ab->...pb", cos_outer, shaped_im, precision=PRECISE)
    turned_re = first_re * twiddle_cos - first_im * rotation_sine
    turned_im = first_re * rotation_sine + first_im * twiddle_cos
    final_re = jnp.matmul(turned_re, cos_inner, precision=PRECISE) - jnp.matmul(
        turned_im, sin_inner, precision=PRECISE
    )
    final_im = jnp.matmul(turned_re, sin_inner, precision=PRECISE) + jnp.matmul(
        turned_im, cos_inner, precision=PRECISE
    )
    final_re = jnp.swapaxes(final_re, -1, -2).reshape(leading + (line_len,))
    final_im = jnp.swapaxes(final_im, -1, -2).reshape(leading + (line_len,))
    return (final_re, final_im)


def swap_slabs(part_re, part_im):
    groups_img = lax.axis_size("img")
    groups_fou = lax.axis_size("fou")
    channels, slab_rows, line_len = part_re.shape

    def pack_blocks(matrix):
        matrix = matrix.reshape(channels, slab_rows, groups_img, groups_fou, slab_rows)
        return matrix.transpose(0, 2, 3, 1, 4).reshape(
            channels, groups_img, groups_fou, slab_rows * slab_rows
        )

    moved_re, moved_im = (
        lax.all_to_all(
            lax.all_to_all(
                for_sending(pack_blocks(part_re)), "img", split_axis=1, concat_axis=1, tiled=True
            ),
            "fou",
            split_axis=2,
            concat_axis=2,
            tiled=True,
        ),
        lax.all_to_all(
            lax.all_to_all(
                for_sending(pack_blocks(part_im)), "img", split_axis=1, concat_axis=1, tiled=True
            ),
            "fou",
            split_axis=2,
            concat_axis=2,
            tiled=True,
        ),
    )

    def unpack_blocks(matrix):
        matrix = matrix.reshape(channels, groups_img * groups_fou, slab_rows, slab_rows)
        return matrix.transpose(0, 3, 1, 2).reshape(channels, slab_rows, line_len)

    return (unpack_blocks(moved_re), unpack_blocks(moved_im))


def band_matrix(filter_taps, out_len):
    taps_len = filter_taps.shape[1]
    offset = (
        jnp.arange(out_len + taps_len - 1, dtype=jnp.int32)[:, None]
        - jnp.arange(out_len, dtype=jnp.int32)[None, :]
    )
    picker = (offset[None, :, :] == jnp.arange(taps_len, dtype=jnp.int32)[:, None, None]).astype(
        jnp.float32
    )
    return jnp.einsum("kt,tjs->kjs", filter_taps, picker, precision=PRECISE)


def filter_tile(padded, filter_taps, out_rows, out_cols):
    radius = (filter_taps.shape[1] - 1) // 2
    col_size = min(128, out_cols)
    col_parts = -(-out_cols // col_size)
    row_size = min(128, out_rows)
    row_parts = -(-out_rows // row_size)
    col_span = col_size + 2 * radius
    windows = jnp.stack(
        [
            padded[..., number * col_size : number * col_size + col_span]
            for number in range(col_parts)
        ],
        axis=-2,
    )
    col_band = band_matrix(filter_taps, col_size)
    if padded.ndim == 3:
        across = jnp.einsum("chnj,kjs->ckhns", windows, col_band, precision=PRECISE)
    else:
        across = jnp.einsum("ckhnj,kjs->ckhns", windows, col_band, precision=PRECISE)
    across = across.reshape(across.shape[:3] + (col_parts * col_size,))
    stacked = jnp.stack([across], axis=2)
    row_band = band_matrix(filter_taps, row_size)
    result = jnp.einsum("cknjw,kjr->cknrw", stacked, row_band, precision=PRECISE)
    result = result.reshape(result.shape[:2] + (row_parts * row_size, col_parts * col_size))
    return result


def body(
    sky_estimate,
    dual_coeffs,
    dirty_image,
    filters,
    thresholds,
    facet_rows,
    tile_slots,
    tile_count,
    gram_tiles,
):
    channels, tile_rows, tile_cols = sky_estimate.shape
    flipped = filters[:, ::-1]
    into_slab_rows = lax.all_to_all(
        sky_estimate.astype(jnp.bfloat16), "fou", split_axis=1, concat_axis=2, tiled=True
    ).astype(sky_estimate.dtype)
    row_real, row_imaginary = transform_final_axis(into_slab_rows, None, -1.0)
    col_re, col_im = swap_slabs(row_real, row_imaginary)
    spec_re, spec_im = transform_final_axis(col_re, col_im, -1.0)
    slab_rows = spec_re.shape[1]
    line_len = spec_re.shape[2]
    which_tile = lax.axis_index("fou") * slab_rows // BLOCK
    slot_blocks = lax.dynamic_index_in_dim(gram_tiles, which_tile, 1, keepdims=False).astype(
        jnp.float32
    )
    chosen = lax.dynamic_index_in_dim(tile_slots, which_tile, 1, keepdims=False)
    used_slots = lax.dynamic_index_in_dim(tile_count, which_tile, 1, keepdims=False)
    in_use = (jnp.arange(SLOTS, dtype=jnp.int32)[None, :] < used_slots[:, None]).astype(jnp.float32)
    matches = (chosen[:, :, None] == jnp.arange(BLOCKS, dtype=jnp.int32)[None, None, :]).astype(
        jnp.float32
    )
    selector = matches * in_use[:, :, None]
    masked = slot_blocks * in_use[:, :, None, None]

    def weigh_part(plane_part):
        by_tile = plane_part.reshape(channels, slab_rows, BLOCKS, BLOCK)
        gathered = jnp.einsum("clta,cst->clsa", by_tile, matches, precision=PRECISE)
        product = jnp.einsum("clsa,csab->clsb", gathered, masked, precision=PRECISE)
        return jnp.einsum("clsb,cst->cltb", product, selector, precision=PRECISE).reshape(
            channels, slab_rows, line_len
        )

    weighted_re = weigh_part(spec_re)
    weighted_im = weigh_part(spec_im)
    back_re, back_im = transform_final_axis(weighted_re, weighted_im, 1.0)
    turn_re, turn_im = swap_slabs(back_re, back_im)
    final_re, final_im = transform_final_axis(turn_re, turn_im, 1.0)
    gram_slab = final_re / float(PIXELS * PIXELS)
    gram_image = lax.all_to_all(
        for_sending(gram_slab), "fou", split_axis=2, concat_axis=1, tiled=True
    ).astype(gram_slab.dtype)
    bordered = padded_2(dual_coeffs[:, 1:], (("img", 2), ("fou", 3)), RADIUS)
    pieces = filter_tile(bordered.astype(jnp.float32), flipped, tile_rows, tile_cols)
    synthesis = dual_coeffs[:, 0].astype(jnp.float32) + jnp.sum(pieces, axis=1)
    live_rows = (jnp.arange(tile_rows, dtype=jnp.int32) < facet_rows[0]).astype(jnp.float32)
    image_next = (
        jnp.maximum(sky_estimate - STEP_PRIMAL * (gram_image - dirty_image + synthesis), 0.0)
        * live_rows[None, :, None]
    )
    probe = 2.0 * image_next - sky_estimate
    beside_all = padded_2(probe, (("img", 1), ("fou", 2)), RADIUS)
    coeffs = filter_tile(beside_all, filters, tile_rows, tile_cols)
    analysis = jnp.concatenate([probe[:, None], coeffs], axis=1)
    candidate = dual_coeffs.astype(jnp.float32) + STEP_DUAL * analysis
    magnitude = jnp.sqrt(jnp.sum(candidate * candidate, axis=0))
    bounds = thresholds[:, None, None]
    dual_next = (candidate * (bounds / jnp.maximum(magnitude, bounds))).astype(jnp.bfloat16)
    return (image_next, dual_next)


def solution(mesh):
    in_specs = (
        P(None, "img", "fou"),
        P(None, None, "img", "fou"),
        P(None, "img", "fou"),
        P(),
        P(),
        P("img"),
        P(None, "img", None),
        P(None, "img"),
        P(None, "img", None, None, None),
    )
    out_specs = (P(None, "img", "fou"), P(None, None, "img", "fou"))
    return jax.shard_map(body, mesh=mesh, in_specs=in_specs, out_specs=out_specs, check_vma=False)
```

profile of v0, /device:TPU:0, one launch (start us, length us, event | category | flops | bytes accessed | tf_op | source)
XLA Modules:
  0.0 628.6 jit_solution(17179058295095508187)
XLA Ops:
  8.9 14.4 %all-to-all-done = bf16[4,128,1024]{2,0,1:T(4,128)(2,1)S(1)} async-done(((bf16[4,128,1024]{2,0,1:T(4,128)(2,1)}), bf16[4,128,1024]{2,0,1:T(4,128)(2,1)S(1)}, u32[]{:S(2)}, u32[]{:S(2)}) %all-to-all-start) | async-done | bytes 1048608 | tf_op jit(solution)/shard_map/all_to_all | solution.py:174
  43.1 6.4 %all-to-all-start.1 = ((bf16[4,16,2,4096]{3,2,0,1:T(2,128)(2,1)}), bf16[4,16,2,4096]{3,2,0,1:T(2,128)(2,1)}, u32[]{:S(2)}, u32[]{:S(2)}) async-start(bf16[4,16,2,4096]{3,2,0,1:T(2,128)(2,1)} %reshape.203), calls=%async_computation.1 | async-start | bytes 2097152 | tf_op jit(solution)/shard_map/all_to_all | solution.py:96
  65.2 7.2 %all-to-all-done.1 = bf16[4,16,2,4096]{3,2,0,1:T(2,128)(2,1)} async-done(((bf16[4,16,2,4096]{3,2,0,1:T(2,128)(2,1)}), bf16[4,16,2,4096]{3,2,0,1:T(2,128)(2,1)}, u32[]{:S(2)}, u32[]{:S(2)}) %all-to-all-start.1) | async-done | bytes 1048608 | tf_op jit(solution)/shard_map/all_to_all | solution.py:96
  72.4 6.8 %all-to-all-start.3 = ((bf16[4,16,2,4096]{3,2,0,1:T(2,128)(2,1)}), bf16[4,16,2,4096]{3,2,0,1:T(2,128)(2,1)S(1)}, u32[]{:S(2)}, u32[]{:S(2)}) async-start(bf16[4,16,2,4096]{3,2,0,1:T(2,128)(2,1)} %reshape.204), calls=%async_computation.3 | async-start | bytes 2097152 | tf_op jit(solution)/shard_map/all_to_all | solution.py:105
  86.7 8.4 %slice.110 = bf16[4,8,128,1024]{3,2,1,0:T(8,128)(2,1)} slice(bf16[4,9,128,1024]{3,2,1,0:T(8,128)(2,1)} %param.10), slice={[0:4], [1:9], [0:128], [0:1024]} | slice | bytes 16777216 | tf_op jit(solution)/shard_map/slice | solution.py:212
  95.7 8.3 %copy.272 = bf16[4,8,128,1024]{3,2,0,1:T(8,128)(2,1)} copy(bf16[4,8,128,1024]{3,2,1,0:T(8,128)(2,1)} %slice.110) | data formatting | bytes 16777216
  113.8 11.7 %all-to-all-done.2 = bf16[4,16,2,4096]{3,1,0,2:T(8,128)(2,1)S(1)} async-done(((bf16[4,16,2,4096]{3,1,0,2:T(8,128)(2,1)}), bf16[4,16,2,4096]{3,1,0,2:T(8,128)(2,1)S(1)}, u32[]{:S(2)}, u32[]{:S(2)}) %all-to-all-start.2) | async-done | bytes 1048608 | tf_op jit(solution)/shard_map/all_to_all | solution.py:95
  138.6 5.8 all-to-all-done.4
  166.8 6.5 %copy.153 = f32[4,64,32,64]{3,2,1,0:T(8,128)} copy(f32[4,64,32,64]{1,3,2,0:T(8,128)} %bitcast.442) | data formatting | bytes 4194304 | tf_op jit(solution)/shard_map/reshape;reshape | solution.py:196
  181.1 5.4 convolution_bitcast_fusion.3
  191.0 5.0 fusion.159
  207.6 6.3 %copy.158 = f32[4,64,32,64]{3,2,1,0:T(8,128)} copy(f32[4,64,32,64]{1,3,2,0:T(8,128)} %bitcast.443) | data formatting | bytes 4194304 | tf_op jit(solution)/shard_map/reshape;reshape | solution.py:196
  219.6 5.4 convolution_bitcast_fusion.2
  252.2 5.1 all-to-all-start.5
  257.3 8.8 %pad_maximum_fusion = bf16[4,8,144,1024]{3,2,0,1:T(8,128)(2,1)} fusion(bf16[4,8,8,1024]{3,2,0,1:T(8,128)(2,1)} %collective-permute-done.1, bf16[4,8,128,1024]{3,2,0,1:T(8,128)(2,1)} %copy.272, bf16[4,8,8,1024]{3,2,0,1:T(8,128)(2,1)} %collective-permute-done), kind=kLoop, calls=%fused_computation.7 | loop fusion | flops 28311552 | bytes 18874368 | tf_op jit(solution)/shard_map/concatenate | solution.py:31
  285.4 19.8 %concatenate.20 = bf16[4,8,144,1040]{3,2,0,1:T(8,128)(2,1)} concatenate(bf16[4,8,144,8]{3,2,0,1:T(8,128)(2,1)S(1)} %copy.184, bf16[4,8,144,1024]{3,2,0,1:T(8,128)(2,1)} %pad_maximum_fusion, bf16[4,8,144,8]{3,2,0,1:T(8,128)(2,1)} %copy.185), dimensions={3} | concatenate | bytes 19169280 | tf_op jit(solution)/shard_map/concatenate | solution.py:31
  305.1 5.2 convert_element_type.275
  331.2 5.9 all-to-all-start.7
  337.1 5.0 fusion.13
  356.9 5.0 fusion.9
  395.5 5.5 all-to-all-done.8
  416.6 10.7 %copy.271 = bf16[4,64,2048]{1,0,2:T(4,128)(2,1)} copy(bf16[4,64,2048]{1,2,0:T(8,128)(2,1)S(1)} %bitcast.453) | data formatting | bytes 2097152 | tf_op jit(solution)/shard_map/convert_element_type | solution.py:22
  435.4 36.3 %convolution_bitcast_fusion.1 = f32[4,8,144,8,128]{4,2,3,0,1:T(8,128)S(1)} fusion(f32[4,8,144,8,144]{4,2,3,0,1:T(8,128)} %fusion.7, f32[8,144,128,1,1]{2,0,1,4,3:T(8,128)S(1)} %bitcast.458), kind=kOutput, calls=%fused_computation.10 | convolution fusion | flops 8153726976 | bytes 40697856 | tf_op jit(solution)/shard_map/ckhnj,kjs->ckhns/dot_general | solution.py:152
  471.7 9.0 %copy.227 = f32[4,8,144,8,128]{4,3,1,2,0:T(8,128)} copy(f32[4,8,144,8,128]{4,2,3,0,1:T(8,128)S(1)} %convolution_bitcast_fusion.1) | data formatting | bytes 37748736 | tf_op jit(solution)/shard_map/reshape.2
  480.6 20.2 %reshape.207 = f32[4,8,144,1024]{3,1,2,0:T(8,128)} reshape(f32[4,8,144,8,128]{4,3,1,2,0:T(8,128)} %copy.227) | data formatting | bytes 37748736 | tf_op jit(solution)/shard_map/reshape.2
  511.2 16.8 %multiply_subtract_fusion = (f32[4,128,1024]{2,1,0:T(8,128)S(1)}, f32[4,128,1024]{2,1,0:T(8,128)}) fusion(f32[4,128,1024]{2,1,0:T(8,128)S(1)} %copy-done.17, f32[128]{0:T(128)S(1)} %compare_convert_fusion, f32[4,8,144,1024]{3,1,2,0:T(8,128)} %reshape.207, f32[144,128,8]{1,2,0:T(8,128)S(1)} %copy-done.19, f32[4,128,1024]{2,1,0:T(8,128)S(1)} %copy-done.20, ...), kind=kOutput, calls=%fused_computation.69 | convolution fusion | flops 7253000192 | bytes 30999040 | tf_op jit(solution)/shard_map/cknjw,kjr->cknrw/dot_general | solution.py:156
  550.0 18.2 %convolution_bitcast_fusion = f32[8,4,8,18,8,128]{5,4,3,2,1,0:T(8,128)} fusion(f32[4,144,8,144]{3,1,0,2:T(8,128)S(1)} %fusion.80, f32[8,144,128,1,1]{2,0,1,4,3:T(8,128)S(1)} %bitcast.456), kind=kOutput, calls=%fused_computation.9 | convolution fusion | flops 8153726976 | bytes 22118400 | tf_op jit(solution)/shard_map/chnj,kjs->ckhns/dot_general | solution.py:150
  568.1 23.8 %fusion.4 = f32[4,8,128,1024]{3,2,0,1:T(8,128)} fusion(f32[8,4,8,18,8,128]{5,4,3,2,1,0:T(8,128)} %convolution_bitcast_fusion, f32[8,144,128,1]{2,0,1,3:T(8,128)} %bitcast.457), kind=kOutput, calls=%fused_computation.8 | convolution fusion | flops 7247757312 | bytes 36241408 | tf_op jit(solution)/shard_map/cknjw,kjr->cknrw/dot_general | solution.py:156
  592.0 11.1 %multiply_reduce_fusion = f32[9,128,1024]{2,1,0:T(8,128)} fusion(f32[4,8,128,1024]{3,2,0,1:T(8,128)} %fusion.4, f32[4,1,128,1024]{3,2,0,1:T(8,128)} %bitcast.440, bf16[4,9,128,1024]{3,2,1,0:T(8,128)(2,1)S(1)} %bitcast.439), kind=kLoop, calls=%fused_computation.6 | loop fusion | flops 27131904 | bytes 33030144 | tf_op jit(solution)/shard_map/reduce_sum | solution.py:225
  603.1 6.9 %maximum_divide_fusion = f32[9,128,1024]{2,1,0:T(8,128)} fusion(f32[9,128,1024]{2,1,0:T(8,128)} %multiply_reduce_fusion, f32[9]{0:T(128)S(1)} %copy-done.27), kind=kLoop, calls=%fused_computation.29 | loop fusion | flops 2359296 | bytes 9437220 | tf_op jit(solution)/shard_map/div | solution.py:227
  610.0 9.0 %multiply_convert_fusion = bf16[4,9,128,1024]{3,2,0,1:T(8,128)(2,1)} fusion(f32[9,128,1024]{2,1,0:T(8,128)} %maximum_divide_fusion, f32[4,8,128,1024]{3,2,0,1:T(8,128)S(1)} %copy-done.2, f32[4,1,128,1024]{3,2,0,1:T(8,128)} %bitcast.441, bf16[4,9,128,1024]{3,2,1,0:T(8,128)(2,1)S(1)} %bitcast.439), kind=kLoop, calls=%fused_computation.5 | loop fusion | flops 28311552 | bytes 42467328 | tf_op jit(solution)/shard_map/convert_element_type | solution.py:227
  618.9 9.3 %copy.202 = bf16[4,9,128,1024]{3,2,1,0:T(8,128)(2,1)} copy(bf16[4,9,128,1024]{3,2,0,1:T(8,128)(2,1)} %multiply_convert_fusion) | data formatting | bytes 18874368
  (199 shorter events, 297.2 us)
Async XLA Ops:
  0.6 103.5 %copy-start = (s32[4,2,6]{2,1,0:T(2,128)S(1)}, s32[4,2,6]{2,1,0:T(2,128)}, u32[]{:S(2)}) copy-start(s32[4,2,6]{2,1,0:T(2,128)} %param.15) | copy-start | bytes 580
  4.6 18.7 %all-to-all-start = ((bf16[4,128,1024]{2,0,1:T(4,128)(2,1)}), bf16[4,128,1024]{2,0,1:T(4,128)(2,1)S(1)}, u32[]{:S(2)}, u32[]{:S(2)}) async-start(bf16[4,128,1024]{2,0,1:T(4,128)(2,1)} %copy.264), calls=%async_computation | async-start | bytes 2097152 | tf_op jit(solution)/shard_map/all_to_all | solution.py:174
  43.1 29.3 %all-to-all-start.1 = ((bf16[4,16,2,4096]{3,2,0,1:T(2,128)(2,1)}), bf16[4,16,2,4096]{3,2,0,1:T(2,128)(2,1)}, u32[]{:S(2)}, u32[]{:S(2)}) async-start(bf16[4,16,2,4096]{3,2,0,1:T(2,128)(2,1)} %reshape.203), calls=%async_computation.1 | async-start | bytes 2097152 | tf_op jit(solution)/shard_map/all_to_all | solution.py:96
  72.4 34.6 %all-to-all-start.3 = ((bf16[4,16,2,4096]{3,2,0,1:T(2,128)(2,1)}), bf16[4,16,2,4096]{3,2,0,1:T(2,128)(2,1)S(1)}, u32[]{:S(2)}, u32[]{:S(2)}) async-start(bf16[4,16,2,4096]{3,2,0,1:T(2,128)(2,1)} %reshape.204), calls=%async_computation.3 | async-start | bytes 2097152 | tf_op jit(solution)/shard_map/all_to_all | solution.py:105
  81.6 175.8 %collective-permute-start.1 = (bf16[4,8,8,1024]{3,2,0,1:T(8,128)(2,1)}, bf16[4,8,8,1024]{3,2,0,1:T(8,128)(2,1)}, u32[]{:S(2)}, u32[]{:S(2)}) collective-permute-start(bf16[4,8,8,1024]{3,2,0,1:T(8,128)(2,1)} %get-tuple-element.13), channel_id=1, source_target_pairs={{2,0},{4,2},{6,4},{8,6},{10,8},{12,10},{14,12},{16,14},{18,16},{20... | collective-permute-start | bytes 1572872 | tf_op jit(solution)/shard_map/ppermute | solution.py:35
  82.8 174.5 %collective-permute-start = (bf16[4,8,8,1024]{3,2,0,1:T(8,128)(2,1)}, bf16[4,8,8,1024]{3,2,0,1:T(8,128)(2,1)}, u32[]{:S(2)}, u32[]{:S(2)}) collective-permute-start(bf16[4,8,8,1024]{3,2,0,1:T(8,128)(2,1)} %get-tuple-element.12), channel_id=1, source_target_pairs={{0,2},{2,4},{4,6},{6,8},{8,10},{10,12},{12,14},{14,16},{16,18},{18... | collective-permute-start | bytes 1572872 | tf_op jit(solution)/shard_map/ppermute | solution.py:33
  95.7 8.3 %copy-start.25 = (f32[8,17]{1,0:T(8,128)S(1)}, f32[8,17]{1,0:T(8,128)}, u32[]{:S(2)}) copy-start(f32[8,17]{1,0:T(8,128)} %param.12) | copy-start | bytes 1636
  107.0 18.5 %all-to-all-start.2 = ((bf16[4,16,2,4096]{3,1,0,2:T(8,128)(2,1)}), bf16[4,16,2,4096]{3,1,0,2:T(8,128)(2,1)S(1)}, u32[]{:S(2)}, u32[]{:S(2)}) async-start(bf16[4,16,2,4096]{3,1,0,2:T(8,128)(2,1)} %copy.143), calls=%async_computation.2 | async-start | bytes 2097152 | tf_op jit(solution)/shard_map/all_to_all | solution.py:95
  125.5 18.9 %all-to-all-start.4 = ((bf16[4,16,2,4096]{3,1,0,2:T(8,128)(2,1)}), bf16[4,16,2,4096]{3,1,0,2:T(8,128)(2,1)}, u32[]{:S(2)}, u32[]{:S(2)}) async-start(bf16[4,16,2,4096]{3,1,0,2:T(8,128)(2,1)} %copy.149), calls=%async_computation.4 | async-start | bytes 2097152 | tf_op jit(solution)/shard_map/all_to_all | solution.py:104
  252.2 79.0 %all-to-all-start.5 = ((bf16[4,16,2,4096]{3,2,0,1:T(2,128)(2,1)}), bf16[4,16,2,4096]{3,2,0,1:T(2,128)(2,1)}, u32[]{:S(2)}, u32[]{:S(2)}) async-start(bf16[4,16,2,4096]{3,2,0,1:T(2,128)(2,1)} %reshape.205), calls=%async_computation.5 | async-start | bytes 2097152 | tf_op jit(solution)/shard_map/all_to_all | solution.py:96
  271.1 5.6 collective-permute-start.2
  275.2 7.8 %collective-permute-start.3 = (bf16[4,8,144,8]{2,3,1,0:T(8,128)(2,1)}, bf16[4,8,144,8]{2,3,1,0:T(8,128)(2,1)}, u32[]{:S(2)}, u32[]{:S(2)}) collective-permute-start(bf16[4,8,144,8]{2,3,1,0:T(8,128)(2,1)} %copy.183), channel_id=1, source_target_pairs={{1,0},{3,2},{5,4},{7,6},{9,8},{11,10},{13,12},{15,14},{17,16},{19,... | collective-permute-start | bytes 221192 | tf_op jit(solution)/shard_map/ppermute | solution.py:35
  310.3 9.2 %copy-start.3 = (f32[4,8,144,1040]{3,2,0,1:T(8,128)}, f32[4,8,144,1040]{3,2,0,1:T(8,128)S(1)}, u32[]{:S(2)}) copy-start(f32[4,8,144,1040]{3,2,0,1:T(8,128)S(1)} %convert_element_type.275) | copy-start | bytes 57507844
  331.2 33.5 %all-to-all-start.7 = ((bf16[4,16,2,4096]{3,2,0,1:T(2,128)(2,1)}), bf16[4,16,2,4096]{3,2,0,1:T(2,128)(2,1)S(1)}, u32[]{:S(2)}, u32[]{:S(2)}) async-start(bf16[4,16,2,4096]{3,2,0,1:T(2,128)(2,1)} %reshape.206), calls=%async_computation.7 | async-start | bytes 2097152 | tf_op jit(solution)/shard_map/all_to_all | solution.py:105
  364.7 18.1 %all-to-all-start.6 = ((bf16[4,16,2,4096]{3,1,0,2:T(8,128)(2,1)}), bf16[4,16,2,4096]{3,1,0,2:T(8,128)(2,1)S(1)}, u32[]{:S(2)}, u32[]{:S(2)}) async-start(bf16[4,16,2,4096]{3,1,0,2:T(8,128)(2,1)} %copy.165), calls=%async_computation.6 | async-start | bytes 2097152 | tf_op jit(solution)/shard_map/all_to_all | solution.py:95
  382.8 18.2 %all-to-all-start.8 = ((bf16[4,16,2,4096]{3,1,0,2:T(8,128)(2,1)}), bf16[4,16,2,4096]{3,1,0,2:T(8,128)(2,1)}, u32[]{:S(2)}, u32[]{:S(2)}) async-start(bf16[4,16,2,4096]{3,1,0,2:T(8,128)(2,1)} %copy.171), calls=%async_computation.8 | async-start | bytes 2097152 | tf_op jit(solution)/shard_map/all_to_all | solution.py:104
  427.3 8.1 %copy-start.19 = (f32[144,128,8]{1,2,0:T(8,128)S(1)}, f32[144,128,8]{1,2,0:T(8,128)}, u32[]{:S(2)}) copy-start(f32[144,128,8]{1,2,0:T(8,128)} %fusion.41) | copy-start | bytes 1769476
  431.0 69.8 %all-to-all-start.9 = ((bf16[2,2,131072]{2,1,0:T(2,128)(2,1)}), bf16[2,2,131072]{2,1,0:T(2,128)(2,1)}, u32[]{:S(2)}, u32[]{:S(2)}) async-start(bf16[2,2,131072]{2,1,0:T(2,128)(2,1)} %reshape.209), calls=%async_computation.9 | async-start | bytes 2097152 | tf_op jit(solution)/shard_map/all_to_all | solution.py:209
  528.0 21.6 %copy-start.4 = (f32[4,128,1024]{2,1,0:T(8,128)}, f32[4,128,1024]{2,1,0:T(8,128)S(1)}, u32[]{:S(2)}) copy-start(f32[4,128,1024]{2,1,0:T(8,128)S(1)} %get-tuple-element.18) | copy-start | bytes 6291460
  528.0 4.5 collective-permute-start.5
  529.3 8.4 %copy-start.24 = (s32[144,128]{1,0:T(8,128)S(1)}, s32[144,128]{1,0:T(8,128)}, u32[]{:S(2)}) copy-start(s32[144,128]{1,0:T(8,128)} %copy-done.23) | copy-start | bytes 221188
  529.3 8.4 %copy-start.26 = (f32[8,17]{1,0:T(8,128)S(1)}, f32[8,17]{1,0:T(8,128)}, u32[]{:S(2)}) copy-start(f32[8,17]{1,0:T(8,128)} %param.12) | copy-start | bytes 1636
  529.3 4.1 collective-permute-start.4
  533.8 10.4 %collective-permute-start.6 = (f32[4,144,8]{2,1,0:T(8,128)S(1)}, f32[4,144,8]{2,1,0:T(8,128)S(1)}, u32[]{:S(2)}, u32[]{:S(2)}) collective-permute-start(f32[4,144,8]{2,1,0:T(8,128)S(1)} %get-tuple-element.15), channel_id=1, source_target_pairs={{0,1},{2,3},{4,5},{6,7},{8,9},{10,11},{12,13},{14,15},{16,17},{18,... | collective-permute-start | bytes 55304 | tf_op jit(solution)/shard_map/ppermute | solution.py:33
  538.4 11.5 %copy-start.18 = (f32[144,128,8]{1,2,0:T(8,128)}, f32[144,128,8]{1,2,0:T(8,128)S(1)}, u32[]{:S(2)}) copy-start(f32[144,128,8]{1,2,0:T(8,128)S(1)} %fusion.40) | copy-start | bytes 1769476
  538.4 11.2 %collective-permute-start.7 = (f32[4,144,8]{2,1,0:T(8,128)S(1)}, f32[4,144,8]{2,1,0:T(8,128)S(1)}, u32[]{:S(2)}, u32[]{:S(2)}) collective-permute-start(f32[4,144,8]{2,1,0:T(8,128)S(1)} %get-tuple-element.14), channel_id=1, source_target_pairs={{1,0},{3,2},{5,4},{7,6},{9,8},{11,10},{13,12},{15,14},{17,16},{19,... | collective-permute-start | bytes 55304 | tf_op jit(solution)/shard_map/ppermute | solution.py:35
  550.0 42.0 %slice-start = ((s8[9437184]{0:T(1024)(128)(4,1)}), s8[4194304]{0:T(1024)(128)(4,1)S(1)}, s32[]{:S(2)}) async-start(s8[9437184]{0:T(1024)(128)(4,1)} %bitcast.438), calls=%async_computation.10 | async-start | bytes 8388608
  568.1 23.8 %slice-start.1 = ((s8[9437184]{0:T(1024)(128)(4,1)}), s8[4194304]{0:T(1024)(128)(4,1)S(1)}, s32[]{:S(2)}) async-start(s8[9437184]{0:T(1024)(128)(4,1)} %bitcast.438), calls=%async_computation.11 | async-start | bytes 8388608
  568.1 23.8 %slice-start.2 = ((s8[9437184]{0:T(1024)(128)(4,1)}), s8[1048576]{0:T(1024)(128)(4,1)S(1)}, s32[]{:S(2)}) async-start(s8[9437184]{0:T(1024)(128)(4,1)} %bitcast.438), calls=%async_computation.12 | async-start | bytes 2097152
  592.0 11.1 %copy-start.27 = (f32[9]{0:T(128)S(1)}, f32[9]{0:T(128)}, u32[]{:S(2)}) copy-start(f32[9]{0:T(128)} %param.13) | copy-start | bytes 112
  592.0 18.0 %copy-start.2 = (f32[4,8,128,1024]{3,2,0,1:T(8,128)S(1)}, f32[4,8,128,1024]{3,2,0,1:T(8,128)}, u32[]{:S(2)}) copy-start(f32[4,8,128,1024]{3,2,0,1:T(8,128)} %fusion.4) | copy-start | bytes 50331652
  618.9 9.3 %copy-start.1 = (s32[4,2,6]{2,1,0:T(2,128)S(1)}, s32[4,2,6]{2,1,0:T(2,128)}, u32[]{:S(2)}) copy-start(s32[4,2,6]{2,1,0:T(2,128)} %param.15) | copy-start | bytes 580
  (18 other events, 67.3 us)
where the time goes:
time: 641 us; the launch traced here: 629 us
  local copies, waits for them, and re-layouts  265 us (41%)
  matrix products  189 us (29%)
  starting transfers between devices  68.2 us (11%)
  waiting for transfers between devices  62.1 us (10%)
  other arithmetic  41.8 us (7%)
    unnamed x82, local copies, waits for them, and re-layouts  67.6 us
    convert_element_type x14, local copies, waits for them, and re-layouts, for_sending(): a.astype(jnp.bfloat16)  55.8 us
    dot_general x2, matrix products, filter_tile(): jnp.einsum('cknjw,kjr->cknrw', stacked, row_band, precision=PRECISE)  40.6 us
    dot_general x1, matrix products, filter_tile(): jnp.einsum('ckhnj,kjs->ckhns', windows, col_band, precision=PRECISE)  36.3 us
    another operation x2, local copies, waits for them, and re-layouts  29.2 us
    concatenate x1, local copies, waits for them, and re-layouts, padded_2(): jnp.concatenate([lax.ppermute(tail, axis, [(i, (i + 1) % count) for i in...  19.8 us
    dot_general x1, matrix products, filter_tile(): across = jnp.einsum('chnj,kjs->ckhns', windows, col_band, precision=PRECISE)  18.2 us
    all_to_all x2, waiting for transfers between devices, swap_slabs(): lax.all_to_all(lax.all_to_all(for_sending(pack_blocks(part_re)), 'img', s...  14.8 us
  transfers between devices with their start and end apart: 18, of which 11 were waited for; matrix products, arithmetic and copies ran while one was open for 53% of the time, Pallas kernels for 0%

commit v1 on v0

v1 whole, which is shorter than its diff:
```python
import functools
import math

import jax
import jax.numpy as jnp
import numpy as np
from jax import lax
from jax.experimental import pallas as pl
from jax.experimental.pallas import tpu as pltpu
from jax.sharding import PartitionSpec as P

STEP_PRIMAL = 0.5
STEP_DUAL = 0.5
LANES = 128
BF16 = jnp.bfloat16
F32 = jnp.float32


def dot(a, b, dims=((1,), (0,)), **kw):
    return lax.dot_general(a, b, (dims, ((), ())), preferred_element_type=F32, **kw)


def flip_halves(x):
    half = x.shape[-1] // 2
    return jnp.concatenate([x[:, half:], x[:, :half]], axis=1)


def half_sign(rows, lanes, dtype=F32):
    lane = lax.broadcasted_iota(jnp.int32, (rows, lanes), 1)
    return jnp.where(lane < lanes // 2, 1.0, -1.0).astype(dtype)


def tables(line, block):
    small = np.arange(block)[:, None] * np.arange(line)[None, :] % line
    angle = small * (2.0 * math.pi / line)
    by_row = np.concatenate([np.cos(angle), np.sin(angle)], axis=0).astype(np.float32)
    period = line // block
    turn = np.arange(period)[:, None] * np.arange(period)[None, :] % period
    turn = turn * (2.0 * math.pi / period)
    return by_row, np.cos(turn).astype(np.float32), np.sin(turn).astype(np.float32)


def turned(base, other, cos_tile, sin_tile):
    rows, lanes = base.shape
    period = cos_tile.shape[0]
    base = base.reshape(rows // period, period, lanes)
    other = other.reshape(rows // period, period, lanes)
    out = base * cos_tile[None] + other * sin_tile[None]
    return out.reshape(rows, lanes).astype(BF16)


def forward_kernel(x_ref, et_ref, es_ref, pc_ref, ps_ref, o_ref):
    both = [turned(et_ref[...], es_ref[...], pc_ref[i], ps_ref[i]) for i in range(2)]
    lanes = et_ref.shape[1]
    out = dot(x_ref[...], jnp.concatenate(both, axis=1))
    sign = half_sign(1, lanes)
    for i in range(2):
        o_ref[i] = (out[:, i * lanes : (i + 1) * lanes] * sign).astype(BF16)


def forward(x, et, es, pc, ps):
    rows, line = x.shape
    tiles, period, lanes = pc.shape
    whole = pl.BlockSpec((line, lanes), lambda i: (0, 0))
    turn = pl.BlockSpec((2, period, lanes), lambda i: (i, 0, 0))
    return pl.pallas_call(
        forward_kernel,
        grid=(tiles // 2,),
        in_specs=[pl.BlockSpec((rows, line), lambda i: (0, 0)), whole, whole, turn, turn],
        out_specs=pl.BlockSpec((2, rows, lanes), lambda i: (i, 0, 0)),
        out_shape=jax.ShapeDtypeStruct((tiles, rows, lanes), BF16),
        name="forward",
    )(x, et, es, pc, ps)


def backward_kernel(scale, y_ref, et_ref, es_ref, pc_ref, ps_ref, o_ref, all_y, table):
    tiles, rows, lanes = y_ref.shape

    @pl.when(pl.program_id(0) == 0)
    def _():
        sign = half_sign(1, lanes)
        for q in range(tiles):
            all_y[:, q * lanes : (q + 1) * lanes] = (y_ref[q].astype(F32) * sign).astype(BF16)

    for q in range(tiles):
        table[:, q * lanes : (q + 1) * lanes] = turned(
            et_ref[...], es_ref[...], pc_ref[q], ps_ref[q]
        )
    out = dot(all_y[...], table[...], ((1,), (1,)))
    o_ref[...] = (out * scale).astype(BF16)


def backward(y, et, es, pc, ps, scale):
    tiles, rows, lanes = y.shape
    line = et.shape[0]
    part = min(256, line)
    chunk = pl.BlockSpec((part, lanes), lambda i: (i, 0))
    fixed = pl.BlockSpec(pc.shape, lambda i: (0, 0, 0))
    return pl.pallas_call(
        functools.partial(backward_kernel, scale),
        grid=(line // part,),
        in_specs=[pl.BlockSpec((tiles, rows, lanes), lambda i: (0, 0, 0)), chunk, chunk, fixed, fixed],
        out_specs=pl.BlockSpec((rows, part), lambda i: (0, i)),
        out_shape=jax.ShapeDtypeStruct((rows, line), BF16),
        scratch_shapes=[
            pltpu.VMEM((rows, tiles * lanes), BF16),
            pltpu.VMEM((part, tiles * lanes), BF16),
        ],
        name="backward",
    )(y, et, es, pc, ps)


def gram_kernel(slots_ref, x_ref, g_ref, e_ref, et_ref, es_ref, rc_ref, rs_ref, pc_ref, ps_ref,
                o_ref, table, table_t):
    c = pl.program_id(0)
    parts, _, rows, lanes = x_ref.shape
    wide, line = e_ref.shape
    block = wide // 2
    slots = g_ref.shape[1]
    x = x_ref[:, 0].reshape(parts * rows, lanes)
    top, low = e_ref[:block], e_ref[block:]
    for k in range(slots):
        t = slots_ref[c, k]
        cos_row = rc_ref[pl.ds(t, 1), :]
        sin_row = rs_ref[pl.ds(t, 1), :]
        table[k * wide : k * wide + block] = (top * cos_row - low * sin_row).astype(BF16)
        table[k * wide + block : (k + 1) * wide] = (low * cos_row + top * sin_row).astype(BF16)
        table_t[:, k * wide : (k + 1) * wide] = turned(
            et_ref[...], es_ref[...], pc_ref[t], ps_ref[t]
        )
    first = dot(table[...], x)
    sign = half_sign(1, lanes)
    stack = []
    for k in range(slots):
        cos_part = first[k * wide : k * wide + block]
        sin_part = first[k * wide + block : (k + 1) * wide]
        spec = cos_part + flip_halves(sin_part) * sign
        out = dot(g_ref[0, k], spec, precision=lax.Precision.HIGHEST)
        stack += [out, flip_halves(out) * -sign]
    stack = jnp.concatenate(stack, axis=0)
    high = stack.astype(BF16)
    low_part = (stack - high.astype(F32)).astype(BF16)
    back = dot(table_t[...], high) + dot(table_t[...], low_part)
    o_ref[:, 0] = back.astype(BF16).reshape(parts, rows, lanes)


def gram(x, slots, g_t, e, et, es, rc, rs, pc, ps):
    parts, channels, rows, lanes = x.shape
    wide, line = e.shape
    count = g_t.shape[1]

    def fixed(a):
        return pl.BlockSpec(a.shape, lambda i, s: (0,) * a.ndim)

    data = pl.BlockSpec((parts, 1, rows, lanes), lambda i, s: (0, i, 0, 0))
    return pl.pallas_call(
        gram_kernel,
        grid_spec=pltpu.PrefetchScalarGridSpec(
            num_scalar_prefetch=1,
            grid=(channels,),
            in_specs=[
                data,
                pl.BlockSpec((1,) + g_t.shape[1:], lambda i, s: (i, 0, 0, 0)),
                fixed(e), fixed(et), fixed(es), fixed(rc), fixed(rs), fixed(pc), fixed(ps),
            ],
            out_specs=data,
            scratch_shapes=[
                pltpu.VMEM((count * wide, line), BF16),
                pltpu.VMEM((line, count * wide), BF16),
            ],
        ),
        out_shape=jax.ShapeDtypeStruct(x.shape, BF16),
        name="gram",
    )(slots, x, g_t, e, et, es, rc, rs, pc, ps)


def synthesis_kernel(d_ref, col_ref, row_ref, o_ref, across):
    _, frames, rows, cols = d_ref.shape
    parts = cols // LANES
    for f in range(frames):
        zero = jnp.zeros((rows, LANES), BF16)
        windows = [jnp.concatenate([zero, d_ref[0, f, :, :LANES]], axis=1)]
        for j in range(1, parts):
            windows.append(d_ref[0, f, :, (j - 1) * LANES : (j + 1) * LANES])
        windows.append(jnp.concatenate([d_ref[0, f, :, cols - LANES :], zero], axis=1))
        out = dot(jnp.concatenate(windows, axis=0), col_ref[f]).astype(BF16)
        for j in range(parts + 1):
            across[f * rows : (f + 1) * rows, j * LANES : (j + 1) * LANES] = out[
                j * rows : (j + 1) * rows
            ]
    o_ref[0] = dot(row_ref[...], across[...])


def synthesize(dual, col_band, row_band):
    channels, frames, rows, cols = dual.shape
    wide = cols + LANES
    tall = row_band.shape[0]
    return pl.pallas_call(
        synthesis_kernel,
        grid=(channels,),
        in_specs=[
            pl.BlockSpec((1, frames, rows, cols), lambda c: (c, 0, 0, 0)),
            pl.BlockSpec(col_band.shape, lambda c: (0, 0, 0)),
            pl.BlockSpec(row_band.shape, lambda c: (0, 0)),
        ],
        out_specs=pl.BlockSpec((1, tall, wide), lambda c: (c, 0, 0)),
        out_shape=jax.ShapeDtypeStruct((channels, tall, wide), F32),
        scratch_shapes=[pltpu.VMEM((frames * rows, wide), BF16)],
        cost_estimate=pl.CostEstimate(
            flops=channels * frames * rows * wide * 800, bytes_accessed=dual.size * 2, transcendentals=0
        ),
        name="synthesis",
    )(dual, col_band, row_band)


def analysis_kernel(bound_ref, p_ref, d_ref, col_ref, row_ref, o_ref, cand):
    channels, _, rows, cols = d_ref.shape
    tall = p_ref.shape[1]
    parts = cols // LANES
    bound = bound_ref[pl.program_id(0)]
    total = None
    for c in range(channels):
        windows = [p_ref[c, :, j * LANES : (j + 2) * LANES] for j in range(parts)]
        out = dot(jnp.concatenate(windows, axis=0), col_ref[0]).astype(BF16)
        across = jnp.concatenate([out[j * tall : (j + 1) * tall] for j in range(parts)], axis=1)
        new = d_ref[c, 0].astype(F32) + STEP_DUAL * dot(row_ref[0], across)
        cand[c] = new
        total = new * new if total is None else total + new * new
    scale = bound / jnp.maximum(jnp.sqrt(total), bound)
    for c in range(channels):
        o_ref[c, 0] = (cand[c] * scale).astype(BF16)


def analyse(probe, dual, col_band, row_band, bounds):
    channels, frames, rows, cols = dual.shape
    block = pl.BlockSpec((channels, 1, rows, cols), lambda f: (0, f, 0, 0))
    return pl.pallas_call(
        analysis_kernel,
        grid=(frames,),
        in_specs=[
            pl.BlockSpec(memory_space=pltpu.SMEM),
            pl.BlockSpec(probe.shape, lambda f: (0, 0, 0)),
            block,
            pl.BlockSpec((1,) + col_band.shape[1:], lambda f: (f, 0, 0)),
            pl.BlockSpec((1,) + row_band.shape[1:], lambda f: (f, 0, 0)),
        ],
        out_specs=block,
        out_shape=jax.ShapeDtypeStruct(dual.shape, BF16),
        scratch_shapes=[pltpu.VMEM((channels, rows, cols), F32)],
        name="analysis",
    )(bounds, probe, dual, col_band, row_band)


def banded(taps, offset):
    count = taps.shape[1]
    out = jnp.zeros((taps.shape[0],) + offset.shape, F32)
    for tap in range(count):
        hit = jnp.asarray(offset) == tap
        out = jnp.where(hit[None], taps[:, tap][:, None, None], out)
    return out.astype(BF16)


def shift_up(x, axis):
    count = lax.axis_size(axis)
    return lax.ppermute(x, axis, [(i, i + 1) for i in range(count - 1)])


def shift_down(x, axis):
    count = lax.axis_size(axis)
    return lax.ppermute(x, axis, [(i + 1, i) for i in range(count - 1)])


def body(sky, dual, dirty, filters, thresholds, facet_rows, tile_slots, tile_count, gram_tiles):
    channels, rows, cols = sky.shape
    taps_len = filters.shape[1]
    radius = (taps_len - 1) // 2
    fou = lax.axis_size("fou")
    img = lax.axis_size("img")
    devices = img * fou
    line = cols * fou
    block = gram_tiles.shape[-1]
    slots = gram_tiles.shape[2]
    tiles = line // block
    slab = rows // fou
    width = line // devices
    axes = ("img", "fou")

    by_row, cos_turn, sin_turn = tables(line, block)
    e = jnp.asarray(by_row)
    et = jnp.asarray(np.ascontiguousarray(by_row.T))
    es = jnp.concatenate([-et[:, block:], et[:, :block]], axis=1)
    lanes = 2 * block
    pc = jnp.broadcast_to(jnp.asarray(cos_turn)[:, :, None], (tiles, tiles, lanes))
    ps = jnp.broadcast_to(jnp.asarray(sin_turn)[:, :, None], (tiles, tiles, lanes))
    rc = jnp.tile(jnp.asarray(cos_turn), (1, line // tiles))
    rs = jnp.tile(jnp.asarray(sin_turn), (1, line // tiles))

    lines = lax.all_to_all(sky.astype(BF16), "fou", split_axis=1, concat_axis=2, tiled=True)
    spread = forward(lines.reshape(channels * slab, line), et, es, pc, ps)
    spread = spread.reshape(tiles, channels, slab, lanes)
    per = block // width
    if per > 1:
        spread = spread.reshape(tiles, channels, slab, 2, per, width)
        spread = spread.transpose(0, 4, 1, 2, 3, 5).reshape(devices, channels, slab, 2 * width)
    moved = lax.all_to_all(spread, axes, split_axis=0, concat_axis=0, tiled=True)

    identity = (jnp.arange(taps_len) == radius).astype(F32)
    taps = jnp.concatenate([identity[None], filters], axis=0)
    frames = taps.shape[0]
    tall = rows + 2 * radius
    near = np.arange(2 * LANES)[:, None]
    synth_col = banded(taps, np.arange(LANES)[None, :] + LANES - near)
    synth_row = banded(taps, np.arange(tall)[:, None] - np.arange(rows)[None, :])
    synth_row = synth_row.transpose(1, 0, 2).reshape(tall, frames * rows)
    ana_col = banded(taps, near - np.arange(LANES)[None, :])
    ana_row = banded(taps, np.arange(tall)[None, :] - np.arange(rows)[:, None])
    ext = synthesize(dual, synth_col, synth_row)
    mid = ext[:, :, radius : radius + cols]
    from_left = shift_up(ext[:, :, radius + cols : cols + 2 * radius], "fou")
    from_right = shift_down(ext[:, :, :radius], "fou")
    rest = cols - radius
    mid = mid + jnp.pad(from_left, ((0, 0), (0, 0), (0, rest))) + jnp.pad(
        from_right, ((0, 0), (0, 0), (rest, 0))
    )
    from_above = shift_up(mid[:, radius + rows :], "img")
    from_below = shift_down(mid[:, :radius], "img")
    rest = rows - radius
    synthesis = (
        mid[:, radius : radius + rows]
        + jnp.pad(from_above, ((0, 0), (0, rest), (0, 0)))
        + jnp.pad(from_below, ((0, 0), (rest, 0), (0, 0)))
    )

    which = lax.axis_index("fou") * width // block
    tile_g = lax.dynamic_index_in_dim(gram_tiles, which, 1, keepdims=False).astype(F32)
    chosen = lax.dynamic_index_in_dim(tile_slots, which, 1, keepdims=False)
    used = lax.dynamic_index_in_dim(tile_count, which, 1, keepdims=False)
    in_use = jnp.arange(slots)[None, :] < used[:, None]
    tile_g = jnp.where(in_use[:, :, None, None], jnp.swapaxes(tile_g, -1, -2), 0.0)

    if slab % 16:
        x = moved.transpose(1, 0, 2, 3).reshape(1, channels, line, 2 * width)
    else:
        x = moved
    y = gram(x, chosen, tile_g, e, et, es, rc, rs, pc, ps)
    if slab % 16:
        y = y.reshape(channels, devices, slab, 2 * width).transpose(1, 0, 2, 3)
    back = lax.all_to_all(y, axes, split_axis=0, concat_axis=0, tiled=True)
    if per > 1:
        back = back.reshape(tiles, per, channels, slab, 2, width).transpose(0, 2, 3, 4, 1, 5)
    back = back.reshape(tiles, channels * slab, lanes)
    final = backward(back, et, es, pc, ps, 1.0 / float(line * line))
    gram_image = lax.all_to_all(
        final.reshape(channels, slab, line), "fou", split_axis=2, concat_axis=1, tiled=True
    ).astype(F32)

    live_rows = (jnp.arange(rows, dtype=jnp.int32) < facet_rows[0]).astype(F32)
    image_next = (
        jnp.maximum(sky - STEP_PRIMAL * (gram_image - dirty + synthesis), 0.0)
        * live_rows[None, :, None]
    )
    probe = (2.0 * image_next - sky).astype(BF16)
    probe = jnp.concatenate(
        [shift_up(probe[:, rows - radius :], "img"), probe, shift_down(probe[:, :radius], "img")],
        axis=1,
    )
    probe = jnp.concatenate(
        [
            shift_up(probe[:, :, cols - radius :], "fou"),
            probe,
            shift_down(probe[:, :, :radius], "fou"),
            jnp.zeros((channels, tall, LANES - 2 * radius), BF16),
        ],
        axis=2,
    )
    dual_next = analyse(probe, dual, ana_col, ana_row, thresholds)
    return (image_next, dual_next)


def solution(mesh):
    in_specs = (
        P(None, "img", "fou"),
        P(None, None, "img", "fou"),
        P(None, "img", "fou"),
        P(),
        P(),
        P("img"),
        P(None, "img", None),
        P(None, "img"),
        P(None, "img", None, None, None),
    )
    out_specs = (P(None, "img", "fou"), P(None, None, "img", "fou"))
    return jax.shard_map(body, mesh=mesh, in_specs=in_specs, out_specs=out_specs, check_vma=False)
```

time: 641 us -> 272 us (0.42); the launches traced: 629 us -> 268 us
  local copies, waits for them, and re-layouts: 265 us -> 52.7 us
  matrix products: 189 us -> 0 us
  Pallas kernels: 0 us -> 81.2 us
  starting transfers between devices: 68.2 us -> 32.8 us
  other arithmetic: 41.8 us -> 20 us
  blocking collectives: 0 us -> 17.7 us
    dot_general x40 -> x0, matrix products: 189 us -> none  [the longest x2 40.6 us: filter_tile(): jnp.einsum('cknjw,kjr->cknrw', stacked, row_band, precision=PRECISE)]
    pallas_call x0 -> x5, Pallas kernels: none -> 81.2 us  [the longest x1 22.5 us: gram(): pl.pallas_call(gram_kernel, grid_spec=pltpu.PrefetchScalarGridSpec(num_sc...]
    convert_element_type x16 -> x2, local copies, waits for them, and re-layouts: 59.6 us -> 5.45 us  [body(): gram_image = lax.all_to_all(final.reshape(channels, slab, line), 'fou', s...]
    another operation x11 -> x4, local copies, waits for them, and re-layouts: 61 us -> 6.98 us  [the longest x2 3.5 us: body(): rc = jnp.tile(jnp.asarray(cos_turn), (1, line // tiles))]
    unnamed x82 -> x266, local copies, waits for them, and re-layouts: 67.6 us -> 23.5 us
    all_to_all x10 -> x3, starting transfers between devices: 49.2 us -> 12.5 us  [the longest x1 5.05 us: body(): lax.all_to_all(spread, axes, split_axis=0, concat_axis=0, tiled=True)]
    all_to_all x0 -> x1, blocking collectives: none -> 17.7 us  [body(): lax.all_to_all(sky.astype(BF16), 'fou', split_axis=1, concat_axis=2, tile...]
    concatenate x1, local copies, waits for them, and re-layouts: 19.8 us -> 2.43 us  [body(): jnp.concatenate([shift_up(probe[:, :, cols - radius:], 'fou'), probe, shi...]
  transfers between devices with their start and end apart: 18 -> 11, of which waited for: 11 -> 2; matrix products, arithmetic and copies ran while one was open for 53% -> 21% of each run, Pallas kernels for 0% -> 9%
where the time goes in v1:
time: 272 us; the launch traced here: 268 us
  Pallas kernels  81.2 us (30%)
  waiting for transfers between devices  60.9 us (22%)
  local copies, waits for them, and re-layouts  52.7 us (19%)
  starting transfers between devices  32.8 us (12%)
  other arithmetic  20 us (7%)
  blocking collectives  17.7 us (7%)
  between operations  3.28 us (1%)
    all_to_all x1, waiting for transfers between devices, body(): lax.all_to_all(spread, axes, split_axis=0, concat_axis=0, tiled=True)  39.7 us
    unnamed x266, local copies, waits for them, and re-layouts  23.5 us
    pallas_call x1, Pallas kernels, gram(): pl.pallas_call(gram_kernel, grid_spec=pltpu.PrefetchScalarGridSpec(num_sc...  22.5 us
    all_to_all x1, waiting for transfers between devices, body(): back = lax.all_to_all(y, axes, split_axis=0, concat_axis=0, tiled=True)  21.2 us
    pallas_call x1, Pallas kernels, analyse(): pl.pallas_call(analysis_kernel, grid=(frames,), in_specs=[pl.BlockSpec(me...  20.9 us
    all_to_all x1, blocking collectives, body(): lax.all_to_all(sky.astype(BF16), 'fou', split_axis=1, concat_axis=2, tile...  17.7 us
    ppermute x4, starting transfers between devices, shift_up(): return lax.ppermute(x, axis, [(i, i + 1) for i in range(count - 1)])  14.9 us
    pallas_call x1, Pallas kernels, backward(): pl.pallas_call(functools.partial(backward_kernel, scale), grid=(line // p...  13.8 us
  transfers between devices with their start and end apart: 11, of which 2 were waited for; matrix products, arithmetic and copies ran while one was open for 21% of the time, Pallas kernels for 9%

profile of v1, /device:TPU:0, one launch (start us, length us, event | category | flops | bytes accessed | tf_op | source)
XLA Modules:
  0.0 268.5 jit_solution(4252570966602152627)
XLA Ops:
  0.6 3.0 %copy.73 = bf16[4,128,1024]{2,0,1:T(4,128)(2,1)S(1)} copy(f32[4,128,1024]{2,1,0:T(8,128)} %param.17) | data formatting | bytes 3145728 | tf_op args[0]
  3.7 17.7 %all_to_all.34 = bf16[4,128,1024]{2,0,1:T(4,128)(2,1)S(1)} all-to-all(bf16[4,128,1024]{2,0,1:T(4,128)(2,1)S(1)} %copy.73), channel_id=1, replica_groups=mesh['img'=16,'fou'=2] {'fou'}, dimensions={1} | all-to-all | bytes 2097152 | tf_op jit(solution)/shard_map/all_to_all | solution.py:298
  25.7 12.9 %forward.1 = bf16[32,256,128]{2,1,0:T(8,128)(2,1)} custom-call(bf16[256,2048]{1,0:T(8,128)(2,1)} %bitcast.153, f32[2048,128]{1,0:T(8,128)} %constant.59.clone.et_ref, f32[2048,128]{1,0:T(8,128)} %constant.72.es_ref, f32[32,32,128]{2,1,0:T(8,128)} %broadcast_in_dim.906.pc_ref, f32[32,32,128]{2,1,0:T(8,128)} %broadcast_in_dim.907.ps_ref), custom_call_target="tpu_custom_call" | custom-call | tf_op jit(solution)/shard_map/forward/pallas_call | solution.py:66
  38.6 5.0 %all-to-all-start.1 = ((bf16[32,4,64,128]{3,2,1,0:T(8,128)(2,1)}), bf16[32,4,64,128]{3,2,1,0:T(8,128)(2,1)S(1)}, u32[]{:S(2)}, u32[]{:S(2)}) async-start(bf16[32,4,64,128]{3,2,1,0:T(8,128)(2,1)} %bitcast.146), calls=%async_computation.1 | async-start | bytes 4194304 | tf_op jit(solution)/shard_map/all_to_all | solution.py:305
  45.0 2.5 tile.9.rc_ref
  48.5 2.4 tile.21.rs_ref
  52.6 39.7 %all-to-all-done.1.x_ref = bf16[32,4,64,128]{3,2,1,0:T(8,128)(2,1)S(1)} async-done(((bf16[32,4,64,128]{3,2,1,0:T(8,128)(2,1)}), bf16[32,4,64,128]{3,2,1,0:T(8,128)(2,1)S(1)}, u32[]{:S(2)}, u32[]{:S(2)}) %all-to-all-start.1) | async-done | bytes 2097184 | tf_op jit(solution)/shard_map/all_to_all | solution.py:305
  93.7 22.5 %gram.1 = bf16[32,4,64,128]{3,2,1,0:T(8,128)(2,1)} custom-call(s32[4,6]{1,0:T(4,128)} %bitcast.205, bf16[32,4,64,128]{3,2,1,0:T(8,128)(2,1)} %copy-done.4, f32[4,6,64,64]{3,2,1,0:T(8,128)} %fusion.7.g_ref, f32[128,2048]{1,0:T(8,128)} %constant.58.clone.e_ref, f32[2048,128]{1,0:T(8,128)} %constant.59.clone.et_ref, f32[2048,128]{1,0:T(8,128)} %constant.72.es_ref, ...), custom_call_target="tpu_custom_call" | custom-call | tf_op jit(solution)/shard_map/gram/pallas_call | solution.py:156
  116.4 3.8 %all-to-all-start.2 = ((bf16[32,4,64,128]{3,2,1,0:T(8,128)(2,1)}), bf16[32,4,64,128]{3,2,1,0:T(8,128)(2,1)S(1)}, u32[]{:S(2)}, u32[]{:S(2)}) async-start(bf16[32,4,64,128]{3,2,1,0:T(8,128)(2,1)} %gram.1), calls=%async_computation.2 | async-start | bytes 4194304 | tf_op jit(solution)/shard_map/all_to_all | solution.py:348
  121.9 2.9 %select_convert_fusion.2.col_ref = bf16[9,256,128]{2,1,0:T(8,128)(2,1)} fusion(bf16[9]{0:T(256)(128)(2,1)S(1)} %get-tuple-element.17, bf16[9]{0:T(256)(128)(2,1)S(1)} %get-tuple-element.18, bf16[9]{0:T(256)(128)(2,1)S(1)} %get-tuple-element.16, bf16[9]{0:T(256)(128)(2,1)S(1)} %get-tuple-element.15, bf16[9]{0:T(256)(128)(2,1)S(1)} %get-tuple-element.14, ...), kind=kLoop, calls=%fused_computation.15 | loop fusion | flops 5013504 | bytes 1147186 | tf_op jit(solution)/shard_map/convert_element_type | solution.py:260
  126.7 2.3 select_convert_fusion.3.row_ref
  129.0 11.1 %synthesis.1 = f32[4,144,1152]{2,1,0:T(8,128)} custom-call(bf16[4,9,128,1024]{3,2,1,0:T(8,128)(2,1)} %d_ref.3, bf16[9,256,128]{2,1,0:T(8,128)(2,1)} %select_convert_fusion.2.col_ref, bf16[144,1152]{1,0:T(8,128)(2,1)} %select_convert_fusion.3.row_ref), custom_call_target="tpu_custom_call" | custom-call | flops 4246732800 | bytes 9437184 | tf_op jit(solution)/shard_map/synthesis/pallas_call | solution.py:198
  140.1 2.0 fusion.43
  142.0 4.2 %collective-permute-start = (f32[4,144,8]{2,1,0:T(8,128)}, f32[4,144,8]{2,1,0:T(8,128)}, u32[]{:S(2)}, u32[]{:S(2)}) collective-permute-start(f32[4,144,8]{2,1,0:T(8,128)} %get-tuple-element.21), channel_id=1, source_target_pairs={{0,1},{2,3},{4,5},{6,7},{8,9},{10,11},{12,13},{14,15},{16,17},{18,... | collective-permute-start | bytes 55304 | tf_op jit(solution)/shard_map/ppermute | solution.py:265
  147.6 21.2 %all-to-all-done.2 = bf16[32,4,64,128]{3,2,1,0:T(8,128)(2,1)S(1)} async-done(((bf16[32,4,64,128]{3,2,1,0:T(8,128)(2,1)}), bf16[32,4,64,128]{3,2,1,0:T(8,128)(2,1)S(1)}, u32[]{:S(2)}, u32[]{:S(2)}) %all-to-all-start.2) | async-done | bytes 2097184 | tf_op jit(solution)/shard_map/all_to_all | solution.py:348
  170.0 13.8 %backward.1 = bf16[256,2048]{1,0:T(8,128)(2,1)} custom-call(bf16[32,256,128]{2,1,0:T(8,128)(2,1)} %bitcast.145, f32[2048,128]{1,0:T(8,128)} %constant.59.clone.et_ref, f32[2048,128]{1,0:T(8,128)} %constant.72.es_ref, f32[32,32,128]{2,1,0:T(8,128)} %broadcast_in_dim.906.pc_ref, f32[32,32,128]{2,1,0:T(8,128)} %broadcast_in_dim.907.ps_ref), custom_call_target="tpu_custom_call" | custom-call | tf_op jit(solution)/shard_map/backward/pallas_call | solution.py:99
  183.8 2.9 %copy.33 = bf16[4,64,2048]{1,0,2:T(4,128)(2,1)S(1)} copy(bf16[4,64,2048]{2,1,0:T(8,128)(2,1)} %bitcast.150) | data formatting | bytes 2097152 | tf_op jit(solution)/shard_map/reshape | solution.py:354
  186.7 2.4 reshape.214
  189.2 3.6 %all-to-all-start.3 = ((bf16[2,2,131072]{2,1,0:T(2,128)(2,1)}), bf16[2,2,131072]{2,1,0:T(2,128)(2,1)S(1)}, u32[]{:S(2)}, u32[]{:S(2)}) async-start(bf16[2,2,131072]{2,1,0:T(2,128)(2,1)} %reshape.214), calls=%async_computation.3 | async-start | bytes 2097152 | tf_op jit(solution)/shard_map/all_to_all | solution.py:353
  193.0 2.6 fusion
  197.8 1.5 collective-permute-start.3
  211.3 2.3 reshape.215
  213.6 2.9 %copy.34 = bf16[4,64,2048]{2,1,0:T(8,128)(2,1)S(1)} copy(bf16[4,64,2048]{1,0,2:T(4,128)(2,1)} %bitcast.148) | data formatting | bytes 2097152 | tf_op jit(solution)/shard_map/all_to_all | solution.py:353
  216.5 3.1 %reshape.196 = f32[4,64,2,1024]{3,2,1,0:T(2,128)} reshape(bf16[4,64,2048]{2,1,0:T(8,128)(2,1)S(1)} %copy.34) | data formatting | bytes 3145728 | tf_op jit(solution)/shard_map/convert_element_type | solution.py:355
  219.6 2.4 copy.35
  222.4 3.3 %subtract_convert_fusion = (bf16[4,128,1024]{2,1,0:T(8,128)(2,1)S(1)}, f32[4,128,1024]{2,1,0:T(8,128)}) fusion(f32[4,128,1024]{2,1,0:T(8,128)S(1)} %copy-done.3, f32[128]{0:T(128)} %compare_convert_fusion, f32[4,8,1024]{2,1,0:T(8,128)} %collective-permute-done.3, f32[4,8,1024]{2,1,0:T(8,128)S(1)} %collective-permute-done.2, f32[4,144,1024]{2,1,0:T(8,128)S(1)} %fusion, ...), kind=kLoop, calls=%fused_computation.11 | loop fusion | flops 5767168 | bytes 11796992 | tf_op jit(solution)/shard_map/convert_element_type | solution.py:362
  226.0 4.7 %collective-permute-start.4 = (bf16[4,8,1024]{2,1,0:T(8,128)(2,1)S(1)}, bf16[4,8,1024]{2,1,0:T(8,128)(2,1)S(1)}, u32[]{:S(2)}, u32[]{:S(2)}) collective-permute-start(bf16[4,8,1024]{2,1,0:T(8,128)(2,1)S(1)} %get-tuple-element.27), channel_id=1, source_target_pairs={{0,2},{2,4},{4,6},{6,8},{8,10},{10,12},{12,14},{14,16},{16,18},{18... | collective-permute-start | bytes 196616 | tf_op jit(solution)/shard_map/ppermute | solution.py:265
  232.2 3.6 %select_convert_fusion.row_ref = bf16[9,128,144]{2,1,0:T(8,128)(2,1)} fusion(bf16[9]{0:T(256)(128)(2,1)S(1)} %copy-done.99, bf16[9]{0:T(256)(128)(2,1)S(1)} %copy-done.101, bf16[9]{0:T(256)(128)(2,1)S(1)} %copy-done.97, bf16[9]{0:T(256)(128)(2,1)S(1)} %copy-done.95, bf16[9]{0:T(256)(128)(2,1)S(1)} %get-tuple-element.14, ...), kind=kLoop, calls=%fused_computation.13 | loop fusion | flops 2820096 | bytes 645426 | tf_op jit(solution)/shard_map/convert_element_type | solution.py:260
  237.4 4.6 %collective-permute-start.6 = (bf16[4,144,8]{2,1,0:T(8,128)(2,1)S(1)}, bf16[4,144,8]{2,1,0:T(8,128)(2,1)S(1)}, u32[]{:S(2)}, u32[]{:S(2)}) collective-permute-start(bf16[4,144,8]{2,1,0:T(8,128)(2,1)S(1)} %get-tuple-element.26), channel_id=1, source_target_pairs={{0,1},{2,3},{4,5},{6,7},{8,9},{10,11},{12,13},{14,15},{16,17},{18,... | collective-permute-start | bytes 27656 | tf_op jit(solution)/shard_map/ppermute | solution.py:265
  242.2 2.9 %select_convert_fusion.1.col_ref = bf16[9,256,128]{2,1,0:T(8,128)(2,1)} fusion(bf16[9]{0:T(256)(128)(2,1)S(1)} %copy-done.99, bf16[9]{0:T(256)(128)(2,1)S(1)} %copy-done.101, bf16[9]{0:T(256)(128)(2,1)S(1)} %copy-done.97, bf16[9]{0:T(256)(128)(2,1)S(1)} %copy-done.95, bf16[9]{0:T(256)(128)(2,1)S(1)} %get-tuple-element.14, ...), kind=kLoop, calls=%fused_computation.14 | loop fusion | flops 5013504 | bytes 1147186 | tf_op jit(solution)/shard_map/convert_element_type | solution.py:260
  245.1 2.4 concatenate.15.p_ref
  247.5 20.9 %analysis.1 = bf16[4,9,128,1024]{3,2,1,0:T(8,128)(2,1)} custom-call(f32[9]{0:T(128)} %bound_ref.1, bf16[4,144,1152]{2,1,0:T(8,128)(2,1)} %concatenate.15.p_ref, bf16[4,9,128,1024]{3,2,1,0:T(8,128)(2,1)} %d_ref.3, bf16[9,256,128]{2,1,0:T(8,128)(2,1)} %select_convert_fusion.1.col_ref, bf16[9,128,144]{2,1,0:T(8,128)(2,1)} %select_convert_fusion.row_ref), custom_call_target="tpu_custom_call" | custom-call | tf_op jit(solution)/shard_map/analysis/pallas_call | solution.py:237
  (321 shorter events, 32.1 us)
Async XLA Ops:
  0.6 43.1 %copy-start = (bf16[4,2,6,64,64]{4,3,2,1,0:T(8,128)(2,1)S(1)}, bf16[4,2,6,64,64]{4,3,2,1,0:T(8,128)(2,1)}, u32[]{:S(2)}) copy-start(bf16[4,2,6,64,64]{4,3,2,1,0:T(8,128)(2,1)} %param.25) | copy-start | bytes 1179652
  38.6 53.7 %all-to-all-start.1 = ((bf16[32,4,64,128]{3,2,1,0:T(8,128)(2,1)}), bf16[32,4,64,128]{3,2,1,0:T(8,128)(2,1)S(1)}, u32[]{:S(2)}, u32[]{:S(2)}) async-start(bf16[32,4,64,128]{3,2,1,0:T(8,128)(2,1)} %bitcast.146), calls=%async_computation.1 | async-start | bytes 4194304 | tf_op jit(solution)/shard_map/all_to_all | solution.py:305
  116.4 52.3 %all-to-all-start.2 = ((bf16[32,4,64,128]{3,2,1,0:T(8,128)(2,1)}), bf16[32,4,64,128]{3,2,1,0:T(8,128)(2,1)S(1)}, u32[]{:S(2)}, u32[]{:S(2)}) async-start(bf16[32,4,64,128]{3,2,1,0:T(8,128)(2,1)} %gram.1), calls=%async_computation.2 | async-start | bytes 4194304 | tf_op jit(solution)/shard_map/all_to_all | solution.py:348
  142.0 50.9 %collective-permute-start = (f32[4,144,8]{2,1,0:T(8,128)}, f32[4,144,8]{2,1,0:T(8,128)}, u32[]{:S(2)}, u32[]{:S(2)}) collective-permute-start(f32[4,144,8]{2,1,0:T(8,128)} %get-tuple-element.21), channel_id=1, source_target_pairs={{0,1},{2,3},{4,5},{6,7},{8,9},{10,11},{12,13},{14,15},{16,17},{18,... | collective-permute-start | bytes 55304 | tf_op jit(solution)/shard_map/ppermute | solution.py:265
  146.3 46.7 %collective-permute-start.1 = (f32[4,144,8]{2,1,0:T(8,128)}, f32[4,144,8]{2,1,0:T(8,128)}, u32[]{:S(2)}, u32[]{:S(2)}) collective-permute-start(f32[4,144,8]{2,1,0:T(8,128)} %get-tuple-element.22), channel_id=1, source_target_pairs={{1,0},{3,2},{5,4},{7,6},{9,8},{11,10},{13,12},{15,14},{17,16},{19,... | collective-permute-start | bytes 55304 | tf_op jit(solution)/shard_map/ppermute | solution.py:270
  189.2 22.1 %all-to-all-start.3 = ((bf16[2,2,131072]{2,1,0:T(2,128)(2,1)}), bf16[2,2,131072]{2,1,0:T(2,128)(2,1)S(1)}, u32[]{:S(2)}, u32[]{:S(2)}) async-start(bf16[2,2,131072]{2,1,0:T(2,128)(2,1)} %reshape.214), calls=%async_computation.3 | async-start | bytes 2097152 | tf_op jit(solution)/shard_map/all_to_all | solution.py:353
  192.9 16.5 %copy-start.60 = (pred[128,144]{1,0:T(32,128)(4,1)S(1)}, pred[128,144]{1,0:T(32,128)(4,1)}, u32[]{:S(2)}) copy-start(pred[128,144]{1,0:T(32,128)(4,1)} %constant.219) | copy-start | bytes 55300
  192.9 17.1 %copy-start.59 = (pred[128,144]{1,0:T(32,128)(4,1)S(1)}, pred[128,144]{1,0:T(32,128)(4,1)}, u32[]{:S(2)}) copy-start(pred[128,144]{1,0:T(32,128)(4,1)} %constant.220) | copy-start | bytes 55300
  196.3 25.8 %collective-permute-start.2 = (f32[4,8,1024]{2,1,0:T(8,128)}, f32[4,8,1024]{2,1,0:T(8,128)S(1)}, u32[]{:S(2)}, u32[]{:S(2)}) collective-permute-start(f32[4,8,1024]{2,1,0:T(8,128)} %get-tuple-element.23), channel_id=1, source_target_pairs={{0,2},{2,4},{4,6},{6,8},{8,10},{10,12},{12,14},{14,16},{16,18},{18... | collective-permute-start | bytes 393224 | tf_op jit(solution)/shard_map/ppermute | solution.py:265
  197.8 24.4 %collective-permute-start.3 = (f32[4,8,1024]{2,1,0:T(8,128)}, f32[4,8,1024]{2,1,0:T(8,128)}, u32[]{:S(2)}, u32[]{:S(2)}) collective-permute-start(f32[4,8,1024]{2,1,0:T(8,128)} %get-tuple-element.24), channel_id=1, source_target_pairs={{2,0},{4,2},{6,4},{8,6},{10,8},{12,10},{14,12},{16,14},{18,16},{20... | collective-permute-start | bytes 393224 | tf_op jit(solution)/shard_map/ppermute | solution.py:270
  225.7 16.2 %copy-start.25 = (pred[256,128]{1,0:T(32,128)(4,1)S(1)}, pred[256,128]{1,0:T(32,128)(4,1)}, u32[]{:S(2)}) copy-start(pred[256,128]{1,0:T(32,128)(4,1)} %constant.203) | copy-start | bytes 98308
  225.8 16.2 %copy-start.26 = (pred[256,128]{1,0:T(32,128)(4,1)S(1)}, pred[256,128]{1,0:T(32,128)(4,1)}, u32[]{:S(2)}) copy-start(pred[256,128]{1,0:T(32,128)(4,1)} %constant.202) | copy-start | bytes 98308
  225.8 16.2 %copy-start.27 = (pred[256,128]{1,0:T(32,128)(4,1)S(1)}, pred[256,128]{1,0:T(32,128)(4,1)}, u32[]{:S(2)}) copy-start(pred[256,128]{1,0:T(32,128)(4,1)} %constant.201) | copy-start | bytes 98308
  225.8 16.2 %copy-start.28 = (pred[256,128]{1,0:T(32,128)(4,1)S(1)}, pred[256,128]{1,0:T(32,128)(4,1)}, u32[]{:S(2)}) copy-start(pred[256,128]{1,0:T(32,128)(4,1)} %constant.200) | copy-start | bytes 98308
  225.8 16.2 %copy-start.29 = (pred[256,128]{1,0:T(32,128)(4,1)S(1)}, pred[256,128]{1,0:T(32,128)(4,1)}, u32[]{:S(2)}) copy-start(pred[256,128]{1,0:T(32,128)(4,1)} %constant.199) | copy-start | bytes 98308
  225.8 16.2 %copy-start.30 = (pred[256,128]{1,0:T(32,128)(4,1)S(1)}, pred[256,128]{1,0:T(32,128)(4,1)}, u32[]{:S(2)}) copy-start(pred[256,128]{1,0:T(32,128)(4,1)} %constant.198) | copy-start | bytes 98308
  225.8 16.2 %copy-start.31 = (pred[256,128]{1,0:T(32,128)(4,1)S(1)}, pred[256,128]{1,0:T(32,128)(4,1)}, u32[]{:S(2)}) copy-start(pred[256,128]{1,0:T(32,128)(4,1)} %constant.197) | copy-start | bytes 98308
  225.8 16.2 %copy-start.32 = (pred[256,128]{1,0:T(32,128)(4,1)S(1)}, pred[256,128]{1,0:T(32,128)(4,1)}, u32[]{:S(2)}) copy-start(pred[256,128]{1,0:T(32,128)(4,1)} %constant.196) | copy-start | bytes 98308
  225.8 16.2 %copy-start.33 = (pred[256,128]{1,0:T(32,128)(4,1)S(1)}, pred[256,128]{1,0:T(32,128)(4,1)}, u32[]{:S(2)}) copy-start(pred[256,128]{1,0:T(32,128)(4,1)} %constant.195) | copy-start | bytes 98308
  225.9 16.2 %copy-start.34 = (pred[256,128]{1,0:T(32,128)(4,1)S(1)}, pred[256,128]{1,0:T(32,128)(4,1)}, u32[]{:S(2)}) copy-start(pred[256,128]{1,0:T(32,128)(4,1)} %constant.194) | copy-start | bytes 98308
  225.9 16.2 %copy-start.35 = (pred[256,128]{1,0:T(32,128)(4,1)S(1)}, pred[256,128]{1,0:T(32,128)(4,1)}, u32[]{:S(2)}) copy-start(pred[256,128]{1,0:T(32,128)(4,1)} %constant.193) | copy-start | bytes 98308
  225.9 16.1 %copy-start.36 = (pred[256,128]{1,0:T(32,128)(4,1)S(1)}, pred[256,128]{1,0:T(32,128)(4,1)}, u32[]{:S(2)}) copy-start(pred[256,128]{1,0:T(32,128)(4,1)} %constant.192) | copy-start | bytes 98308
  225.9 16.1 %copy-start.37 = (pred[256,128]{1,0:T(32,128)(4,1)S(1)}, pred[256,128]{1,0:T(32,128)(4,1)}, u32[]{:S(2)}) copy-start(pred[256,128]{1,0:T(32,128)(4,1)} %constant.191) | copy-start | bytes 98308
  225.9 16.1 %copy-start.38 = (pred[256,128]{1,0:T(32,128)(4,1)S(1)}, pred[256,128]{1,0:T(32,128)(4,1)}, u32[]{:S(2)}) copy-start(pred[256,128]{1,0:T(32,128)(4,1)} %constant.190) | copy-start | bytes 98308
  225.9 16.1 %copy-start.39 = (pred[256,128]{1,0:T(32,128)(4,1)S(1)}, pred[256,128]{1,0:T(32,128)(4,1)}, u32[]{:S(2)}) copy-start(pred[256,128]{1,0:T(32,128)(4,1)} %constant.189) | copy-start | bytes 98308
  225.9 16.1 %copy-start.40 = (pred[256,128]{1,0:T(32,128)(4,1)S(1)}, pred[256,128]{1,0:T(32,128)(4,1)}, u32[]{:S(2)}) copy-start(pred[256,128]{1,0:T(32,128)(4,1)} %constant.188) | copy-start | bytes 98308
  225.9 16.1 %copy-start.41 = (pred[256,128]{1,0:T(32,128)(4,1)S(1)}, pred[256,128]{1,0:T(32,128)(4,1)}, u32[]{:S(2)}) copy-start(pred[256,128]{1,0:T(32,128)(4,1)} %constant.187) | copy-start | bytes 98308
  226.0 9.8 %collective-permute-start.4 = (bf16[4,8,1024]{2,1,0:T(8,128)(2,1)S(1)}, bf16[4,8,1024]{2,1,0:T(8,128)(2,1)S(1)}, u32[]{:S(2)}, u32[]{:S(2)}) collective-permute-start(bf16[4,8,1024]{2,1,0:T(8,128)(2,1)S(1)} %get-tuple-element.27), channel_id=1, source_target_pairs={{0,2},{2,4},{4,6},{6,8},{8,10},{10,12},{12,14},{14,16},{16,18},{18... | collective-permute-start | bytes 196616 | tf_op jit(solution)/shard_map/ppermute | solution.py:265
  230.7 5.1 %collective-permute-start.5 = (bf16[4,8,1024]{2,1,0:T(8,128)(2,1)S(1)}, bf16[4,8,1024]{2,1,0:T(8,128)(2,1)S(1)}, u32[]{:S(2)}, u32[]{:S(2)}) collective-permute-start(bf16[4,8,1024]{2,1,0:T(8,128)(2,1)S(1)} %get-tuple-element.28), channel_id=1, source_target_pairs={{2,0},{4,2},{6,4},{8,6},{10,8},{12,10},{14,12},{16,14},{18,16},{20... | collective-permute-start | bytes 196616 | tf_op jit(solution)/shard_map/ppermute | solution.py:270
  236.1 9.0 %collective-permute-start.7 = (bf16[4,144,8]{2,1,0:T(8,128)(2,1)S(1)}, bf16[4,144,8]{2,1,0:T(8,128)(2,1)S(1)}, u32[]{:S(2)}, u32[]{:S(2)}) collective-permute-start(bf16[4,144,8]{2,1,0:T(8,128)(2,1)S(1)} %get-tuple-element.25), channel_id=1, source_target_pairs={{1,0},{3,2},{5,4},{7,6},{9,8},{11,10},{13,12},{15,14},{17,16},{19,... | collective-permute-start | bytes 27656 | tf_op jit(solution)/shard_map/ppermute | solution.py:270
  237.4 7.7 %collective-permute-start.6 = (bf16[4,144,8]{2,1,0:T(8,128)(2,1)S(1)}, bf16[4,144,8]{2,1,0:T(8,128)(2,1)S(1)}, u32[]{:S(2)}, u32[]{:S(2)}) collective-permute-start(bf16[4,144,8]{2,1,0:T(8,128)(2,1)S(1)} %get-tuple-element.26), channel_id=1, source_target_pairs={{0,1},{2,3},{4,5},{6,7},{8,9},{10,11},{12,13},{14,15},{16,17},{18,... | collective-permute-start | bytes 27656 | tf_op jit(solution)/shard_map/ppermute | solution.py:265
  247.5 21.0 %copy-start.1 = (bf16[4,2,6,64,64]{4,3,2,1,0:T(8,128)(2,1)S(1)}, bf16[4,2,6,64,64]{4,3,2,1,0:T(8,128)(2,1)}, u32[]{:S(2)}) copy-start(bf16[4,2,6,64,64]{4,3,2,1,0:T(8,128)(2,1)} %param.25) | copy-start | bytes 1179652
  (101 other events, 728.5 us)
